TPU v7x, 32 devices: a whole 2x2x4 slice. The times are simulated.
32 devices in a mesh: grp: 2 (over y), seq: 4 (over z), tp: 2 (over x), pr: 2 (over core).
Axes of the slice: x: 2, y: 2, z: 4, core: 2. Of those that a mesh axis runs over, the one named last changes fastest.
Arguments:
- dna_feats: bfloat16 [2048, 768], P(('grp', 'seq', 'pr'), 'tp'), parts along dimension 0, may hold values from -6 to 6
- conv_w: bfloat16 [5, 768, 1536], P(None, 'pr', 'tp'), may hold values from -0.09375 to 0.09375
- conv_gain: float32 [1536], P('tp'), may hold values from 0.1 to 1.9
- attn_gain: float32 [1536], replicated, may hold values from 0.1 to 1.9
- wq: bfloat16 [1536, 1024], P('pr', 'tp'), as said below
- wk: bfloat16 [1536, 1024], P('pr', 'tp'), as said below
- wv: bfloat16 [1536, 1536], P('pr', 'tp'), may hold values from -0.3125 to 0.3125
- wo: bfloat16 [1536, 1536], P('tp', 'pr'), may hold values from -0.15625 to 0.15625
- pair_w: bfloat16 [1536, 256], P('tp'), may hold values from -0.3125 to 0.3125
- pair_in: bfloat16 [128, 64, 128], P(('grp', 'seq', 'tp'), 'pr'), parts along dimension 0, may hold values from -6 to 6
- pair_gain: float32 [128], replicated, may hold values from 0.1 to 1.9
- pair_w1: bfloat16 [128, 256], replicated, may hold values from -0.5 to 0.5
- pair_w2: bfloat16 [256, 128], replicated, may hold values from -0.375 to 0.375
Outputs:
- trunk: bfloat16 [2048, 1536], P(('grp', 'seq', 'pr'), 'tp'), parts along dimension 0
- pair_out: bfloat16 [128, 64, 128], P(('grp', 'seq', 'tp'), 'pr'), parts along dimension 0
There are 2 independent parts, one for each index of `grp`. A program takes and returns all parts, laid end to end along the dimension named above; an argument that names none is the same for every part. Nothing has to cross between parts.
Inputs may be any that keep to these rules, and one draw needn't show every extreme that they name: `wq`: before rounding to bfloat16, entries lie between -3.5 / sqrt(1536) and 3.5 / sqrt(1536). `wk`: before rounding to bfloat16, entries lie between -8.75 / sqrt(1536) and 8.75 / sqrt(1536).
All inputs are finite; a program needn't handle non-finite values.
Results may differ from a plain program's by a relative error of at most 0.013.
The roundings to bfloat16 on the way count: a program that leaves them out, or rounds other values in their place, can miss the bound.
Values may be sent and summed in bfloat16 or wider, within the bound.
A program may use at most 64 MiB of HBM per device.

v0:
```python
import math
import jax
import jax.numpy as jnp
from jax import lax
from jax.sharding import PartitionSpec as P

QK = 128
HV = 192
POOL = 16
EPSILON = 1e-06


def extended(value, sides, width):
    for axis, dim in sides:
        devices, length = (lax.axis_size(axis), value.shape[dim])
        up = [(i, (i + 1) % devices) for i in range(devices - 1)]
        down = [(j, i) for i, j in up]
        last = lax.slice_in_dim(value, length - width, length, axis=dim)
        first = lax.slice_in_dim(value, 0, width, axis=dim)
        before = lax.ppermute(last, axis, up)
        after = lax.ppermute(first, axis, down)
        value = jnp.concatenate([before, value, after], axis=dim)
    return value


def rms_scale(values):
    return lax.rsqrt(jnp.mean(values * values, axis=-1, keepdims=True) + EPSILON)


def attention_start(query_block):
    head_count = query_block.shape[1]
    row_count = query_block.shape[0]
    highest = jnp.full((head_count, row_count), -1e30, jnp.float32)
    totals = jnp.zeros((head_count, row_count), jnp.float32)
    mixed = jnp.zeros((row_count, head_count, HV), jnp.float32)
    return (highest, totals, mixed)


def attention_step(query_block, carry, pieces):
    factor = 1.0 / math.sqrt(QK)
    highest, totals, mixed = carry
    key_piece, value_piece = pieces
    scores = (
        jnp.einsum("qhd,khd->hqk", query_block, key_piece, preferred_element_type=jnp.float32)
        * factor
    )
    new_high = jnp.maximum(highest, jnp.max(scores, axis=-1))
    weights = jnp.exp(scores - new_high[:, :, None])
    totals = jnp.sum(weights, axis=-1)
    added = jnp.einsum(
        "hqk,khd->qhd",
        weights.astype(jnp.bfloat16),
        value_piece,
        preferred_element_type=jnp.float32,
    )
    mixed = added
    return (new_high, totals, mixed)


def attention_finish(carry):
    highest, totals, mixed = carry
    return (mixed / jnp.transpose(totals)[:, :, None]).astype(jnp.bfloat16)


def local(
    dna_feats,
    conv_w,
    conv_gain,
    attn_gain,
    wq,
    wk,
    wv,
    wo,
    pair_w,
    pair_in,
    pair_gain,
    pair_w1,
    pair_w2,
):
    row_count = dna_feats.shape[0]
    reach = conv_w.shape[0] // 2
    rimmed = extended(dna_feats, ((("seq", "pr"), 0),), reach)
    channels = lax.all_gather(rimmed, "tp", axis=1, tiled=True)
    conv_empty = jnp.zeros((row_count, conv_w.shape[2]), jnp.float32)
    total = conv_empty
    piece = lax.all_gather(conv_w, "pr", axis=1, tiled=True)
    sliced = channels
    for offset in range(piece.shape[0]):
        total = total + jnp.dot(
            sliced[offset : offset + row_count], piece[offset], preferred_element_type=jnp.float32
        )
    squares = lax.psum(jnp.sum(total * total, axis=1, keepdims=True), "tp")
    model_width = total.shape[1] * lax.axis_size("tp")
    hidden_conv = jax.nn.gelu(
        total * lax.rsqrt(squares / model_width + EPSILON) * conv_gain
    ).astype(jnp.bfloat16)
    trunk_full = lax.all_gather(hidden_conv, "tp", axis=1, tiled=True)
    trunk_wide = trunk_full.astype(jnp.float32)
    normed = (trunk_wide * rms_scale(trunk_wide) * attn_gain).astype(jnp.bfloat16)
    query_width = wq.shape[1]
    pieces = (
        lax.all_gather(wq, "pr", axis=0, tiled=True),
        lax.all_gather(wk, "pr", axis=0, tiled=True),
        lax.all_gather(wv, "pr", axis=0, tiled=True),
    )
    sliced = normed
    query_sum, key_sum, value_sum = tuple(
        (jnp.dot(sliced, piece, preferred_element_type=jnp.float32) for piece in pieces)
    )
    head_count = query_width // QK
    queries = query_sum.astype(jnp.bfloat16).reshape(row_count, head_count, QK)
    keys_local = key_sum.astype(jnp.bfloat16).reshape(row_count, head_count, QK)
    values_local = value_sum.astype(jnp.bfloat16).reshape(row_count, head_count, HV)
    moved_query, moved_keys, moved_values = (
        lax.all_to_all(queries, "pr", split_axis=1, concat_axis=0, tiled=True),
        lax.all_to_all(keys_local, "pr", split_axis=1, concat_axis=0, tiled=True),
        lax.all_to_all(values_local, "pr", split_axis=1, concat_axis=0, tiled=True),
    )
    carried = attention_step(
        moved_query,
        attention_start(moved_query),
        (
            lax.all_gather(moved_keys, "seq", axis=0, tiled=True),
            lax.all_gather(moved_values, "seq", axis=0, tiled=True),
        ),
    )
    attended = lax.all_to_all(
        attention_finish(carried), "pr", split_axis=0, concat_axis=1, tiled=True
    )
    attended_flat = attended.reshape(row_count, head_count * HV)
    head_terms = jnp.dot(
        attended_flat,
        lax.all_gather(wo, "pr", axis=1, tiled=True),
        preferred_element_type=jnp.float32,
    )
    own_share = lax.psum_scatter(
        head_terms.astype(jnp.bfloat16), "tp", scatter_dimension=1, tiled=True
    ).astype(jnp.float32)
    trunk = (hidden_conv.astype(jnp.float32) + own_share).astype(jnp.bfloat16)
    pooled = trunk.astype(jnp.float32).reshape(row_count // POOL, POOL, -1).mean(axis=1)
    partial_embed = jnp.dot(pooled, pair_w.astype(jnp.float32), precision=lax.Precision.HIGHEST)
    embedded = lax.psum(partial_embed, "tp").astype(jnp.bfloat16)
    every_embed = lax.all_gather(embedded, ("seq", "pr"), axis=0, tiled=True)
    pair_rows = pair_in.shape[0]
    pair_cols = pair_in.shape[1]
    pair_width = pair_in.shape[2]
    row_first = lax.axis_index(("seq", "tp")) * pair_rows
    col_first = lax.axis_index("pr") * pair_cols
    row_embed = lax.dynamic_slice_in_dim(every_embed, row_first, pair_rows, 0)[
        :, :pair_width
    ].astype(jnp.float32)
    col_embed = lax.dynamic_slice_in_dim(every_embed, col_first, pair_cols, 0)[
        :, pair_width:
    ].astype(jnp.float32)
    summed = pair_in.astype(jnp.float32) + row_embed[:, None, :] + col_embed[None, :, :]
    pair_normed = (summed * rms_scale(summed) * pair_gain).astype(jnp.bfloat16)
    inner = jax.nn.gelu(
        jnp.dot(pair_normed.reshape(-1, pair_width), pair_w1, preferred_element_type=jnp.float32)
    ).astype(jnp.bfloat16)
    update = jnp.dot(inner, pair_w2, preferred_element_type=jnp.float32).reshape(summed.shape)
    pair_out = (summed + update).astype(jnp.bfloat16)
    return (trunk, pair_out)


def solution(mesh):
    in_specs = (
        P(("grp", "seq", "pr"), "tp"),
        P(None, "pr", "tp"),
        P("tp"),
        P(),
        P("pr", "tp"),
        P("pr", "tp"),
        P("pr", "tp"),
        P("tp", "pr"),
        P("tp", None),
        P(("grp", "seq", "tp"), "pr", None),
        P(),
        P(),
        P(),
    )
    out_specs = (P(("grp", "seq", "pr"), "tp"), P(("grp", "seq", "tp"), "pr", None))
    return jax.shard_map(local, mesh=mesh, in_specs=in_specs, out_specs=out_specs, check_vma=False)
```

profile of v0, /device:TPU:0, one launch (start us, length us, event | category | flops | bytes accessed | tf_op | source)
XLA Modules:
  0.0 160.2 jit_solution(4517351203953663694)
XLA Ops:
  7.2 0.7 all-gather.6.cloned.1.call-update
  8.0 0.7 all-gather.12.cloned.1.call-update
  8.7 0.7 all-gather.10.cloned.1.call-update
  10.1 2.4 %collective-permute-start = (bf16[2,384]{1,0:T(2,128)(2,1)S(1)}, bf16[2,384]{1,0:T(2,128)(2,1)S(1)}, u32[]{:S(2)}, u32[]{:S(2)}) collective-permute-start(bf16[2,384]{1,0:T(2,128)(2,1)S(1)} %get-tuple-element.4), channel_id=1, source_target_pairs={{0,1},{1,4},{4,5},{5,8},{8,9},{9,12},{12,13},{2,3},{3,6},{6,7},{7,... | collective-permute-start | bytes 4616 | tf_op jit(solution)/shard_map/ppermute | solution.py:20
  12.5 1.3 collective-permute-start.1
  13.8 3.9 %collective-permute-done.1 = bf16[2,384]{1,0:T(2,128)(2,1)S(1)} collective-permute-done((bf16[2,384]{1,0:T(2,128)(2,1)S(1)}, bf16[2,384]{1,0:T(2,128)(2,1)S(1)}, u32[]{:S(2)}, u32[]{:S(2)}) %collective-permute-start.1) | collective-permute-done | bytes 1568 | tf_op jit(solution)/shard_map/ppermute | solution.py:21
  17.7 5.4 %all_gather.30 = bf16[132,768]{1,0:T(8,128)(2,1)S(1)} all-gather(bf16[132,384]{1,0:T(8,128)(2,1)S(1)} %pad_maximum_fusion), channel_id=1, replica_groups=mesh['grp'=2,'seq'=4,'tp'=2,'pr'=2] {'tp'}, dimensions={1}, use_global_device_ids=true | all-gather | bytes 304128 | tf_op jit(solution)/shard_map/all_gather | solution.py:83
  23.1 5.4 %all-gather.6.cloned.1.call-done = bf16[5,768,768]{2,1,0:T(8,128)(2,1)} async-done(((bf16[5,384,768]{2,1,0:T(8,128)(2,1)}), bf16[5,768,768]{2,1,0:T(8,128)(2,1)}) %all-gather.6.cloned.1.call-update) | async-done | bytes 5898256 | tf_op jit(solution)/shard_map/all_gather | solution.py:86
  28.5 1.6 fusion.3
  30.1 1.6 convolution_add_fusion.3
  31.7 1.6 convolution_add_fusion.2
  33.3 1.6 convolution_add_fusion.1
  34.9 1.7 %multiply_reduce_fusion.1 = (f32[128]{0:T(128)S(1)}, f32[128,768]{1,0:T(8,128)S(1)}) fusion(f32[128,768]{1,0:T(8,128)S(1)} %convolution_add_fusion.1, bf16[5,768,768]{2,1,0:T(8,128)(2,1)} %all-gather.6.cloned.1.call-done, bf16[132,768]{1,0:T(8,128)(2,1)S(1)} %all_gather.30), kind=kOutput, calls=%fused_computation.42 | convolution fusion | flops 151289728 | bytes 2163200 | tf_op jit(solution)/shard_map/dot_general | solution.py:89
  36.6 4.9 %psum.14 = f32[128,1]{0,1:T(1,128)S(1)} all-reduce(f32[128,1]{0,1:T(1,128)S(1)} %bitcast.89), channel_id=1, replica_groups=mesh['grp'=2,'seq'=4,'tp'=2,'pr'=2] {'tp'}, use_global_device_ids=true, to_apply=%region_1.0 | all-reduce | flops 128 | bytes 1024 | tf_op jit(solution)/shard_map/psum | solution.py:92
  41.8 6.6 %all_gather.32 = bf16[128,1536]{1,0:T(8,128)(2,1)S(1)} all-gather(bf16[128,768]{1,0:T(8,128)(2,1)S(1)} %fusion.20), channel_id=1, replica_groups=mesh['grp'=2,'seq'=4,'tp'=2,'pr'=2] {'tp'}, dimensions={1}, use_global_device_ids=true | all-gather | bytes 589824 | tf_op jit(solution)/shard_map/all_gather | solution.py:97
  48.6 2.0 %fusion.6 = bf16[16,4,8,128]{3,2,1,0:T(8,128)(2,1)S(1)} fusion(bf16[1536,512]{1,0:T(8,128)(2,1)} %all-gather.12.cloned.1.call-done, bf16[128,1536]{1,0:T(8,128)(2,1)S(1)} %all_gather.32, f32[1536]{0:T(1024)S(1)} %copy-done.3, f32[128]{0:T(128)S(1)} %add_rsqrt_fusion.1), kind=kOutput, calls=%fused_computation.22 | convolution fusion | flops 202178560 | bytes 2103808 | tf_op jit(solution)/shard_map/dot_general | solution.py:108
  50.6 3.8 %all_to_all.69 = bf16[128,4,128]{2,0,1:T(8,128)(2,1)S(1)} all-to-all(bf16[128,4,128]{2,0,1:T(8,128)(2,1)S(1)} %bitcast.82), channel_id=1, replica_groups=mesh['grp'=2,'seq'=4,'tp'=2,'pr'=2] {'pr'}, dimensions={1} | all-to-all | bytes 262144 | tf_op jit(solution)/shard_map/all_to_all | solution.py:116
  54.5 1.8 %fusion.5 = bf16[16,4,8,128]{3,2,1,0:T(8,128)(2,1)S(1)} fusion(bf16[1536,512]{1,0:T(8,128)(2,1)} %all-gather.10.cloned.1.call-done, bf16[128,1536]{1,0:T(8,128)(2,1)S(1)} %all_gather.32, f32[1536]{0:T(1024)S(1)} %copy-done.3, f32[128]{0:T(128)S(1)} %add_rsqrt_fusion.1), kind=kOutput, calls=%fused_computation.21 | convolution fusion | flops 202178560 | bytes 2103808 | tf_op jit(solution)/shard_map/dot_general | solution.py:108
  56.3 3.8 %all_to_all.70 = bf16[128,4,128]{2,0,1:T(8,128)(2,1)S(1)} all-to-all(bf16[128,4,128]{2,0,1:T(8,128)(2,1)S(1)} %bitcast.84), channel_id=1, replica_groups=mesh['grp'=2,'seq'=4,'tp'=2,'pr'=2] {'pr'}, dimensions={1} | all-to-all | bytes 262144 | tf_op jit(solution)/shard_map/all_to_all | solution.py:115
  60.2 6.9 %all-gather.8.cloned.1.call-done = bf16[1536,768]{1,0:T(8,128)(2,1)} async-done(((bf16[768,768]{1,0:T(8,128)(2,1)}), bf16[1536,768]{1,0:T(8,128)(2,1)}) %all-gather.8.cloned.1.call-update) | async-done | bytes 2359312 | tf_op jit(solution)/shard_map/all_gather | solution.py:104
  67.1 2.2 %convolution_convert_fusion.1 = bf16[128,768]{1,0:T(8,128)(2,1)S(1)} fusion(bf16[1536,768]{1,0:T(8,128)(2,1)} %all-gather.8.cloned.1.call-done, bf16[128,1536]{1,0:T(8,128)(2,1)S(1)} %all_gather.32, f32[1536]{0:T(1024)S(1)} %copy-done.3, f32[128]{0:T(128)S(1)} %add_rsqrt_fusion.1), kind=kOutput, calls=%fused_computation.18 | convolution fusion | flops 302874624 | bytes 2955776 | tf_op jit(solution)/shard_map/dot_general | solution.py:108
  69.5 3.9 %all_to_all.71 = bf16[128,4,192]{0,2,1:T(8,128)(2,1)S(1)} all-to-all(bf16[128,4,192]{0,2,1:T(8,128)(2,1)S(1)} %bitcast.77), channel_id=1, replica_groups=mesh['grp'=2,'seq'=4,'tp'=2,'pr'=2] {'pr'}, dimensions={1} | all-to-all | bytes 393216 | tf_op jit(solution)/shard_map/all_to_all | solution.py:117
  73.4 16.1 %all_gather.37 = bf16[1024,2,128]{2,0,1:T(8,128)(2,1)S(1)} all-gather(bf16[256,2,128]{2,0,1:T(8,128)(2,1)S(1)} %bitcast.80), channel_id=1, replica_groups=mesh['grp'=2,'seq'=4,'tp'=2,'pr'=2] {'seq'}, dimensions={0}, use_global_device_ids=true | all-gather | bytes 655360 | tf_op jit(solution)/shard_map/all_gather | solution.py:123
  90.6 18.9 %all_gather.34 = bf16[1024,2,192]{0,2,1:T(8,128)(2,1)S(1)} all-gather(bf16[256,2,192]{0,2,1:T(8,128)(2,1)S(1)} %bitcast.79), channel_id=1, replica_groups=mesh['grp'=2,'seq'=4,'tp'=2,'pr'=2] {'seq'}, dimensions={0}, use_global_device_ids=true | all-gather | bytes 983040 | tf_op jit(solution)/shard_map/all_gather | solution.py:124
  109.5 0.6 fusion.4
  110.3 3.9 %all_to_all.72 = bf16[256,2,192]{2,1,0:T(2,128)(2,1)S(1)} all-to-all(bf16[256,2,192]{2,1,0:T(2,128)(2,1)S(1)} %copy.36), channel_id=1, replica_groups=mesh['grp'=2,'seq'=4,'tp'=2,'pr'=2] {'pr'}, dimensions={0} | all-to-all | bytes 393216 | tf_op jit(solution)/shard_map/all_to_all | solution.py:127
  114.5 3.0 %convolution_convert_fusion = bf16[128,1536]{1,0:T(8,128)(2,1)} fusion(bf16[128,768]{0,1:T(8,128)(2,1)S(1)} %bitcast.76, bf16[768,1536]{1,0:T(8,128)(2,1)} %all-gather.14.cloned.1.call-done), kind=kOutput, calls=%fused_computation | convolution fusion | flops 302186496 | bytes 2949120 | tf_op jit(solution)/shard_map/dot_general | solution.py:131
  117.5 13.2 %reduce-scatter.2.cloned.1.call-done = bf16[128,768]{1,0:T(8,128)(2,1)} async-done(((bf16[128,1536]{1,0:T(8,128)(2,1)}), bf16[128,768]{1,0:T(8,128)(2,1)}) %reduce-scatter.2.cloned.1.call-update) | async-done | bytes 196624 | tf_op jit(solution)/shard_map/reduce_scatter | solution.py:136
  130.7 1.9 %convert_reduce_fusion = (f32[8,768]{1,0:T(8,128)S(1)}, bf16[128,768]{1,0:T(8,128)(2,1)}) fusion(bf16[128,768]{1,0:T(8,128)(2,1)} %reduce-scatter.2.cloned.1.call-done, f32[768]{0:T(1024)S(1)} %copy-done.4, f32[128,768]{1,0:T(8,128)S(1)} %get-tuple-element.7, f32[128]{0:T(128)S(1)} %rsqrt_bitcast_fusion), kind=kLoop, calls=%fused_computation.39 | loop fusion | flops 1665024 | bytes 814592 | tf_op jit(solution)/shard_map/reduce_sum | solution.py:140
  132.9 5.0 %psum.15 = bf16[8,256]{1,0:T(8,128)(2,1)S(1)} all-reduce(f32[8,256]{1,0:T(8,128)S(1)} %fusion.39), channel_id=1, replica_groups=mesh['grp'=2,'seq'=4,'tp'=2,'pr'=2] {'tp'}, use_global_device_ids=true, to_apply=%region_7.0 | all-reduce | flops 2048 | bytes 12288 | tf_op jit(solution)/shard_map/psum | solution.py:142
  137.9 14.1 %all_gather.39 = bf16[64,256]{1,0:T(8,128)(2,1)S(1)} all-gather(bf16[8,256]{1,0:T(8,128)(2,1)S(1)} %psum.15), channel_id=1, replica_groups=mesh['grp'=2,'seq'=4,'tp'=2,'pr'=2] {'seq','pr'}, dimensions={0}, use_global_device_ids=true | all-gather | bytes 36864 | tf_op jit(solution)/shard_map/all_gather | solution.py:143
  152.7 0.7 add_convert_fusion.1
  (53 shorter events, 3.8 us)
Async XLA Ops:
  7.2 125.5 %copy-start = (bf16[768,256]{1,0:T(8,128)(2,1)S(1)}, bf16[768,256]{1,0:T(8,128)(2,1)}, u32[]{:S(2)}) copy-start(bf16[768,256]{1,0:T(8,128)(2,1)} %param.21) | copy-start | bytes 1179652
  7.2 21.3 %all-gather.6.cloned.1.call-start = ((), (), s32[]{:S(2)}) async-start(), calls=%async_computation.5 | async-start | bytes 8847360 | tf_op jit(solution)/shard_map/all_gather | solution.py:86
  7.9 2.1 %copy-start.2 = (bf16[128,384]{1,0:T(8,128)(2,1)S(1)}, bf16[128,384]{1,0:T(8,128)(2,1)}, u32[]{:S(2)}) copy-start(bf16[128,384]{1,0:T(8,128)(2,1)} %param.13) | copy-start | bytes 294916
  7.9 40.7 %all-gather.12.cloned.1.call-start = ((), (), s32[]{:S(2)}) async-start(), calls=%async_computation.8 | async-start | bytes 2359296 | tf_op jit(solution)/shard_map/all_gather | solution.py:103
  8.7 45.8 %all-gather.10.cloned.1.call-start = ((), (), s32[]{:S(2)}) async-start(), calls=%async_computation.7 | async-start | bytes 2359296 | tf_op jit(solution)/shard_map/all_gather | solution.py:102
  9.4 57.7 %all-gather.8.cloned.1.call-start = ((), (), s32[]{:S(2)}) async-start(), calls=%async_computation.6 | async-start | bytes 3538944 | tf_op jit(solution)/shard_map/all_gather | solution.py:104
  10.0 104.5 %all-gather.14.cloned.1.call-start = ((), (), s32[]{:S(2)}) async-start(), calls=%async_computation.9 | async-start | bytes 3538944 | tf_op jit(solution)/shard_map/all_gather | solution.py:133
  10.1 3.8 %collective-permute-start = (bf16[2,384]{1,0:T(2,128)(2,1)S(1)}, bf16[2,384]{1,0:T(2,128)(2,1)S(1)}, u32[]{:S(2)}, u32[]{:S(2)}) collective-permute-start(bf16[2,384]{1,0:T(2,128)(2,1)S(1)} %get-tuple-element.4), channel_id=1, source_target_pairs={{0,1},{1,4},{4,5},{5,8},{8,9},{9,12},{12,13},{2,3},{3,6},{6,7},{7,... | collective-permute-start | bytes 4616 | tf_op jit(solution)/shard_map/ppermute | solution.py:20
  12.5 5.2 %collective-permute-start.1 = (bf16[2,384]{1,0:T(2,128)(2,1)S(1)}, bf16[2,384]{1,0:T(2,128)(2,1)S(1)}, u32[]{:S(2)}, u32[]{:S(2)}) collective-permute-start(bf16[2,384]{1,0:T(2,128)(2,1)S(1)} %get-tuple-element.5), channel_id=1, source_target_pairs={{1,0},{4,1},{5,4},{8,5},{9,8},{12,9},{13,12},{3,2},{6,3},{7,6},{10... | collective-permute-start | bytes 4616 | tf_op jit(solution)/shard_map/ppermute | solution.py:21
  13.8 116.9 %reduce-scatter.2.cloned.1.call-start = ((), (), s32[]{:S(2)}) async-start(), calls=%async_computation.10 | async-start | bytes 589824 | tf_op jit(solution)/shard_map/reduce_scatter | solution.py:136
  33.3 8.3 %copy-start.4 = (f32[768]{0:T(1024)S(1)}, f32[768]{0:T(1024)}, u32[]{:S(2)}) copy-start(f32[768]{0:T(1024)} %param.15) | copy-start | bytes 9220
  34.9 13.7 %copy-start.3 = (f32[1536]{0:T(1024)S(1)}, f32[1536]{0:T(1024)}, u32[]{:S(2)}) copy-start(f32[1536]{0:T(1024)} %param.16) | copy-start | bytes 18436
  114.5 37.5 %copy-start.1 = (bf16[8,32,128]{2,1,0:T(8,128)(2,1)S(1)}, bf16[8,32,128]{2,1,0:T(8,128)(2,1)}, u32[]{:S(2)}) copy-start(bf16[8,32,128]{2,1,0:T(8,128)(2,1)} %param.22) | copy-start | bytes 196612
  114.5 37.7 %copy-start.5 = (f32[128]{0:T(128)S(1)}, f32[128]{0:T(128)}, u32[]{:S(2)}) copy-start(f32[128]{0:T(128)} %param.23) | copy-start | bytes 1540
  114.5 37.8 %copy-start.6 = (bf16[256,128]{1,0:T(8,128)(2,1)S(1)}, bf16[256,128]{1,0:T(8,128)(2,1)}, u32[]{:S(2)}) copy-start(bf16[256,128]{1,0:T(8,128)(2,1)} %param.25) | copy-start | bytes 196612
  114.5 37.8 %copy-start.7 = (bf16[128,256]{1,0:T(8,128)(2,1)S(1)}, bf16[128,256]{1,0:T(8,128)(2,1)}, u32[]{:S(2)}) copy-start(bf16[128,256]{1,0:T(8,128)(2,1)} %param.24) | copy-start | bytes 196612
Sparse Core Ops, SparseCore 0:
  9.5 18.8 all-gather.5
  30.0 10.9 all-gather.11
  42.6 10.9 all-gather.9
  55.0 12.1 all-gather.7
  68.5 12.1 all-gather.13
  117.7 13.0 reduce-scatter.1
where the time goes:
time: 161 us; the launch traced here: 160 us
  blocking collectives  86.6 us (54%)
  waiting for transfers between devices  32 us (20%)
  matrix products  18.8 us (12%)
  between operations  14.4 us (9%)
  starting transfers between devices  3.92 us (2%)
  other arithmetic  3.73 us (2%)
    all_gather x1, blocking collectives, local(): lax.all_gather(moved_values, 'seq', axis=0, tiled=True)  18.9 us
    all_gather x1, blocking collectives, local(): lax.all_gather(moved_keys, 'seq', axis=0, tiled=True)  16.1 us
    all_gather x1, blocking collectives, local(): every_embed = lax.all_gather(embedded, ('seq', 'pr'), axis=0, tiled=True)  14.1 us
    reduce_scatter x1, waiting for transfers between devices, local(): lax.psum_scatter(head_terms.astype(jnp.bfloat16), 'tp', scatter_dimension...  13.2 us
    dot_general x5, matrix products, local(): jnp.dot(sliced[offset:offset + row_count], piece[offset], preferred_eleme...  8.08 us
    all_gather x1, waiting for transfers between devices, local(): lax.all_gather(wv, 'pr', axis=0, tiled=True)  6.94 us
    all_gather x1, blocking collectives, local(): trunk_full = lax.all_gather(hidden_conv, 'tp', axis=1, tiled=True)  6.61 us
    dot_general x3, matrix products, local(): jnp.dot(sliced, piece, preferred_element_type=jnp.float32)  5.97 us
  transfers between devices with their start and end apart: 8, of which 4 were waited for; matrix products, arithmetic and copies ran while one was open for 10% of the time, Pallas kernels for 0%

commit v1 on v0

--- a/solution.py
+++ b/solution.py
@@ -8,6 +8,16 @@
 HV = 192
 POOL = 16
 EPSILON = 1e-06
+
+
+def ring_gather(x, axis, dim):
+    ways, here, step = (lax.axis_size(axis), lax.axis_index(axis), x.shape[dim])
+    shape = [n * ways if d == dim else n for d, n in enumerate(x.shape)]
+    full = lax.dynamic_update_slice_in_dim(jnp.zeros(shape, x.dtype), x, here * step, axis=dim)
+    for far in range(1, ways):
+        x = lax.ppermute(x, axis, [(d, (d + 1) % ways) for d in range(ways)])
+        full = lax.dynamic_update_slice_in_dim(full, x, (here - far) % ways * step, axis=dim)
+    return full
 
 
 def extended(value, sides, width):
@@ -120,7 +130,7 @@
         moved_query,
         attention_start(moved_query),
         (
-            lax.all_gather(moved_keys, "seq", axis=0, tiled=True),
+            ring_gather(moved_keys, "seq", 0),
             lax.all_gather(moved_values, "seq", axis=0, tiled=True),
         ),
     )

time: 161 us -> 156 us (0.969)
  blocking collectives: 86.6 us -> 66.4 us
  starting transfers between devices: 3.92 us -> 11.2 us
  waiting for transfers between devices: 32 us -> 39.1 us
    all_gather x1 -> x0, blocking collectives: 16.1 us -> none  [local(): lax.all_gather(moved_keys, 'seq', axis=0, tiled=True)]
    all_gather x1, waiting for transfers between devices: 0.02 us -> 8.69 us  [local(): lax.all_gather(wq, 'pr', axis=0, tiled=True)]
    all_gather x1, waiting for transfers between devices: 6.94 us -> 0.01 us  [local(): lax.all_gather(wv, 'pr', axis=0, tiled=True)]
    ppermute x0 -> x3, waiting for transfers between devices: none -> 6.62 us  [ring_gather(): x = lax.ppermute(x, axis, [(d, (d + 1) % ways) for d in range(ways)])]
    ppermute x0 -> x3, starting transfers between devices: none -> 3.89 us  [ring_gather(): x = lax.ppermute(x, axis, [(d, (d + 1) % ways) for d in range(ways)])]
    all_to_all x1 -> x0, blocking collectives: 3.84 us -> none  [local(): lax.all_to_all(queries, 'pr', split_axis=1, concat_axis=0, tiled=True)]
    all_to_all x0 -> x1, starting transfers between devices: none -> 3.39 us  [local(): lax.all_to_all(queries, 'pr', split_axis=1, concat_axis=0, tiled=True)]
  transfers between devices with their start and end apart: 8 -> 12, of which waited for: 4 -> 5; matrix products, arithmetic and copies ran while one was open for 10% -> 11% of each run, Pallas kernels for 0% -> 0%
where the time goes in v1:
time: 156 us; the launch traced here: 155 us
  blocking collectives  66.4 us (43%)
  waiting for transfers between devices  39.1 us (25%)
  matrix products  18.8 us (12%)
  between operations  14.5 us (9%)
  starting transfers between devices  11.2 us (7%)
  other arithmetic  3.73 us (2%)
    all_gather x1, blocking collectives, local(): lax.all_gather(moved_values, 'seq', axis=0, tiled=True)  18.6 us
    all_gather x1, blocking collectives, local(): every_embed = lax.all_gather(embedded, ('seq', 'pr'), axis=0, tiled=True)  14.1 us
    reduce_scatter x1, waiting for transfers between devices, local(): lax.psum_scatter(head_terms.astype(jnp.bfloat16), 'tp', scatter_dimension...  12 us
    all_gather x1, waiting for transfers between devices, local(): lax.all_gather(wq, 'pr', axis=0, tiled=True)  8.69 us
    dot_general x5, matrix products, local(): jnp.dot(sliced[offset:offset + row_count], piece[offset], preferred_eleme...  8.08 us
    ppermute x3, waiting for transfers between devices, ring_gather(): x = lax.ppermute(x, axis, [(d, (d + 1) % ways) for d in range(ways)])  6.62 us
    all_gather x1, blocking collectives, local(): trunk_full = lax.all_gather(hidden_conv, 'tp', axis=1, tiled=True)  6.61 us
    dot_general x3, matrix products, local(): jnp.dot(sliced, piece, preferred_element_type=jnp.float32)  6.01 us
  transfers between devices with their start and end apart: 12, of which 5 were waited for; matrix products, arithmetic and copies ran while one was open for 11% of the time, Pallas kernels for 0%

profile of v1, /device:TPU:0, one launch (start us, length us, event | category | flops | bytes accessed | tf_op | source)
XLA Modules:
  0.0 155.3 jit_solution(12905304796393048935)
XLA Ops:
  7.2 0.7 all-gather.6.cloned.1.call-update
  8.0 0.7 all-gather.12.cloned.1.call-update
  8.7 0.7 all-gather.8.cloned.1.call-update
  10.1 2.4 %collective-permute-start = (bf16[2,384]{1,0:T(2,128)(2,1)S(1)}, bf16[2,384]{1,0:T(2,128)(2,1)S(1)}, u32[]{:S(2)}, u32[]{:S(2)}) collective-permute-start(bf16[2,384]{1,0:T(2,128)(2,1)S(1)} %get-tuple-element.4), channel_id=1, source_target_pairs={{0,1},{1,4},{4,5},{5,8},{8,9},{9,12},{12,13},{2,3},{3,6},{6,7},{7,... | collective-permute-start | bytes 4616 | tf_op jit(solution)/shard_map/ppermute | solution.py:30
  12.5 1.3 collective-permute-start.1
  13.9 3.8 %collective-permute-done.1 = bf16[2,384]{1,0:T(2,128)(2,1)S(1)} collective-permute-done((bf16[2,384]{1,0:T(2,128)(2,1)S(1)}, bf16[2,384]{1,0:T(2,128)(2,1)S(1)}, u32[]{:S(2)}, u32[]{:S(2)}) %collective-permute-start.1) | collective-permute-done | bytes 1568 | tf_op jit(solution)/shard_map/ppermute | solution.py:31
  17.7 5.4 %all_gather.27 = bf16[132,768]{1,0:T(8,128)(2,1)S(1)} all-gather(bf16[132,384]{1,0:T(8,128)(2,1)S(1)} %pad_maximum_fusion), channel_id=1, replica_groups=mesh['grp'=2,'seq'=4,'tp'=2,'pr'=2] {'tp'}, dimensions={1}, use_global_device_ids=true | all-gather | bytes 304128 | tf_op jit(solution)/shard_map/all_gather | solution.py:93
  23.1 5.4 %all-gather.6.cloned.1.call-done = bf16[5,768,768]{2,1,0:T(8,128)(2,1)} async-done(((bf16[5,384,768]{2,1,0:T(8,128)(2,1)}), bf16[5,768,768]{2,1,0:T(8,128)(2,1)}) %all-gather.6.cloned.1.call-update) | async-done | bytes 5898256 | tf_op jit(solution)/shard_map/all_gather | solution.py:96
  28.5 1.6 %fusion.2 = f32[128,768]{1,0:T(8,128)S(1)} fusion(bf16[5,768,768]{2,1,0:T(8,128)(2,1)} %all-gather.6.cloned.1.call-done, bf16[132,768]{1,0:T(8,128)(2,1)S(1)} %all_gather.27), kind=kOutput, calls=%fused_computation.14 | convolution fusion | flops 150994944 | bytes 1769472 | tf_op jit(solution)/shard_map/dot_general | solution.py:99
  30.1 1.6 %convolution_add_fusion.3 = f32[128,768]{1,0:T(8,128)S(1)} fusion(f32[128,768]{1,0:T(8,128)S(1)} %fusion.2, bf16[5,768,768]{2,1,0:T(8,128)(2,1)} %all-gather.6.cloned.1.call-done, bf16[132,768]{1,0:T(8,128)(2,1)S(1)} %all_gather.27), kind=kOutput, calls=%fused_computation.9 | convolution fusion | flops 151093248 | bytes 2162688 | tf_op jit(solution)/shard_map/dot_general | solution.py:99
  31.7 1.6 %convolution_add_fusion.2 = f32[128,768]{1,0:T(8,128)S(1)} fusion(f32[128,768]{1,0:T(8,128)S(1)} %convolution_add_fusion.3, bf16[5,768,768]{2,1,0:T(8,128)(2,1)} %all-gather.6.cloned.1.call-done, bf16[132,768]{1,0:T(8,128)(2,1)S(1)} %all_gather.27), kind=kOutput, calls=%fused_computation.8 | convolution fusion | flops 151093248 | bytes 2162688 | tf_op jit(solution)/shard_map/dot_general | solution.py:99
  33.3 1.6 %convolution_add_fusion.1 = f32[128,768]{1,0:T(8,128)S(1)} fusion(f32[128,768]{1,0:T(8,128)S(1)} %convolution_add_fusion.2, bf16[5,768,768]{2,1,0:T(8,128)(2,1)} %all-gather.6.cloned.1.call-done, bf16[132,768]{1,0:T(8,128)(2,1)S(1)} %all_gather.27), kind=kOutput, calls=%fused_computation.7 | convolution fusion | flops 151093248 | bytes 2162688 | tf_op jit(solution)/shard_map/dot_general | solution.py:99
  34.9 1.7 %multiply_reduce_fusion.1 = (f32[128]{0:T(128)S(1)}, f32[128,768]{1,0:T(8,128)S(1)}) fusion(f32[128,768]{1,0:T(8,128)S(1)} %convolution_add_fusion.1, bf16[5,768,768]{2,1,0:T(8,128)(2,1)} %all-gather.6.cloned.1.call-done, bf16[132,768]{1,0:T(8,128)(2,1)S(1)} %all_gather.27), kind=kOutput, calls=%fused_computation.41 | convolution fusion | flops 151289728 | bytes 2163200 | tf_op jit(solution)/shard_map/dot_general | solution.py:99
  36.6 4.9 %psum.14 = f32[128,1]{0,1:T(1,128)S(1)} all-reduce(f32[128,1]{0,1:T(1,128)S(1)} %bitcast.87), channel_id=1, replica_groups=mesh['grp'=2,'seq'=4,'tp'=2,'pr'=2] {'tp'}, use_global_device_ids=true, to_apply=%region_1.0 | all-reduce | flops 128 | bytes 1024 | tf_op jit(solution)/shard_map/psum | solution.py:102
  41.8 6.6 %all_gather.29 = bf16[128,1536]{1,0:T(8,128)(2,1)S(1)} all-gather(bf16[128,768]{1,0:T(8,128)(2,1)S(1)} %fusion.18), channel_id=1, replica_groups=mesh['grp'=2,'seq'=4,'tp'=2,'pr'=2] {'tp'}, dimensions={1}, use_global_device_ids=true | all-gather | bytes 589824 | tf_op jit(solution)/shard_map/all_gather | solution.py:107
  48.6 2.0 %fusion.4 = bf16[16,4,8,128]{3,2,1,0:T(8,128)(2,1)S(1)} fusion(bf16[1536,512]{1,0:T(8,128)(2,1)} %all-gather.12.cloned.1.call-done, bf16[128,1536]{1,0:T(8,128)(2,1)S(1)} %all_gather.29, f32[1536]{0:T(1024)S(1)} %copy-done.3, f32[128]{0:T(128)S(1)} %add_rsqrt_fusion.1), kind=kOutput, calls=%fused_computation.20 | convolution fusion | flops 202178560 | bytes 2103808 | tf_op jit(solution)/shard_map/dot_general | solution.py:118
  50.6 3.9 %all_to_all.69 = bf16[128,4,128]{2,0,1:T(8,128)(2,1)S(1)} all-to-all(bf16[128,4,128]{2,0,1:T(8,128)(2,1)S(1)} %bitcast.82), channel_id=1, replica_groups=mesh['grp'=2,'seq'=4,'tp'=2,'pr'=2] {'pr'}, dimensions={1} | all-to-all | bytes 262144 | tf_op jit(solution)/shard_map/all_to_all | solution.py:126
  54.6 1.8 %collective-permute-start.2 = (bf16[256,2,128]{2,0,1:T(8,128)(2,1)S(1)}, bf16[256,2,128]{2,0,1:T(8,128)(2,1)S(1)}, u32[]{:S(2)}, u32[]{:S(2)}) collective-permute-start(bf16[256,2,128]{2,0,1:T(8,128)(2,1)S(1)} %bitcast.79), channel_id=1, source_target_pairs={{0,4},{4,8},{8,12},{12,0},{1,5},{5,9},{9,13},{13,1},{2,6},{6,10},{... | collective-permute-start | bytes 393224 | tf_op jit(solution)/shard_map/ppermute | solution.py:18
  56.3 2.2 %convolution_convert_fusion.1 = bf16[128,768]{1,0:T(8,128)(2,1)S(1)} fusion(bf16[1536,768]{1,0:T(8,128)(2,1)} %all-gather.8.cloned.1.call-done, bf16[128,1536]{1,0:T(8,128)(2,1)S(1)} %all_gather.29, f32[1536]{0:T(1024)S(1)} %copy-done.3, f32[128]{0:T(128)S(1)} %add_rsqrt_fusion.1), kind=kOutput, calls=%fused_computation.16 | convolution fusion | flops 302874624 | bytes 2955776 | tf_op jit(solution)/shard_map/dot_general | solution.py:118
  58.5 8.7 %all-gather.10.cloned.1.call-done = bf16[1536,512]{1,0:T(8,128)(2,1)} async-done(((bf16[768,512]{1,0:T(8,128)(2,1)}), bf16[1536,512]{1,0:T(8,128)(2,1)}) %all-gather.10.cloned.1.call-update) | async-done | bytes 1572880 | tf_op jit(solution)/shard_map/all_gather | solution.py:112
  67.2 1.8 %fusion.3 = bf16[16,4,8,128]{3,2,1,0:T(8,128)(2,1)S(1)} fusion(bf16[1536,512]{1,0:T(8,128)(2,1)} %all-gather.10.cloned.1.call-done, bf16[128,1536]{1,0:T(8,128)(2,1)S(1)} %all_gather.29, f32[1536]{0:T(1024)S(1)} %copy-done.3, f32[128]{0:T(128)S(1)} %add_rsqrt_fusion.1), kind=kOutput, calls=%fused_computation.19 | convolution fusion | flops 202178560 | bytes 2103808 | tf_op jit(solution)/shard_map/dot_general | solution.py:118
  69.9 3.9 %all_to_all.70 = bf16[128,4,192]{0,2,1:T(8,128)(2,1)S(1)} all-to-all(bf16[128,4,192]{0,2,1:T(8,128)(2,1)S(1)} %bitcast.76), channel_id=1, replica_groups=mesh['grp'=2,'seq'=4,'tp'=2,'pr'=2] {'pr'}, dimensions={1} | all-to-all | bytes 393216 | tf_op jit(solution)/shard_map/all_to_all | solution.py:127
  73.8 3.4 %all-to-all-start.1 = ((bf16[128,4,128]{2,0,1:T(8,128)(2,1)}), bf16[128,4,128]{2,0,1:T(8,128)(2,1)S(1)}, u32[]{:S(2)}, u32[]{:S(2)}) async-start(bf16[128,4,128]{2,0,1:T(8,128)(2,1)} %bitcast.72), calls=%async_computation.1 | async-start | bytes 262144 | tf_op jit(solution)/shard_map/all_to_all | solution.py:125
  77.3 1.8 %collective-permute-start.3 = (bf16[256,2,128]{2,0,1:T(8,128)(2,1)S(1)}, bf16[256,2,128]{2,0,1:T(8,128)(2,1)S(1)}, u32[]{:S(2)}, u32[]{:S(2)}) collective-permute-start(bf16[256,2,128]{2,0,1:T(8,128)(2,1)S(1)} %collective-permute-done.2), channel_id=1, source_target_pairs={{0,4},{4,8},{8,12},{12,0},{1,5},{5,9},{9,13},{13,1},{2,6},{6,10},{... | collective-permute-start | bytes 393224 | tf_op jit(solution)/shard_map/ppermute | solution.py:18
  79.1 18.6 %all_gather.31 = bf16[1024,2,192]{0,2,1:T(8,128)(2,1)S(1)} all-gather(bf16[256,2,192]{0,2,1:T(8,128)(2,1)S(1)} %bitcast.77), channel_id=1, replica_groups=mesh['grp'=2,'seq'=4,'tp'=2,'pr'=2] {'seq'}, dimensions={0}, use_global_device_ids=true | all-gather | bytes 983040 | tf_op jit(solution)/shard_map/all_gather | solution.py:134
  98.2 6.6 %collective-permute-done.4 = bf16[256,2,128]{2,0,1:T(8,128)(2,1)S(1)} collective-permute-done((bf16[256,2,128]{2,0,1:T(8,128)(2,1)S(1)}, bf16[256,2,128]{2,0,1:T(8,128)(2,1)S(1)}, u32[]{:S(2)}, u32[]{:S(2)}) %collective-permute-start.4) | collective-permute-done | bytes 131104 | tf_op jit(solution)/shard_map/ppermute | solution.py:18
  106.8 3.9 %all_to_all.71 = bf16[256,2,192]{2,1,0:T(2,128)(2,1)S(1)} all-to-all(bf16[256,2,192]{2,1,0:T(2,128)(2,1)S(1)} %copy.36), channel_id=1, replica_groups=mesh['grp'=2,'seq'=4,'tp'=2,'pr'=2] {'pr'}, dimensions={0} | all-to-all | bytes 393216 | tf_op jit(solution)/shard_map/all_to_all | solution.py:137
  111.0 3.0 %convolution_convert_fusion = bf16[128,1536]{1,0:T(8,128)(2,1)} fusion(bf16[128,768]{0,1:T(8,128)(2,1)S(1)} %bitcast.74, bf16[768,1536]{1,0:T(8,128)(2,1)} %all-gather.14.cloned.1.call-done), kind=kOutput, calls=%fused_computation | convolution fusion | flops 302186496 | bytes 2949120 | tf_op jit(solution)/shard_map/dot_general | solution.py:141
  114.0 12.0 %reduce-scatter.2.cloned.1.call-done = bf16[128,768]{1,0:T(8,128)(2,1)} async-done(((bf16[128,1536]{1,0:T(8,128)(2,1)}), bf16[128,768]{1,0:T(8,128)(2,1)}) %reduce-scatter.2.cloned.1.call-update) | async-done | bytes 196624 | tf_op jit(solution)/shard_map/reduce_scatter | solution.py:146
  125.9 1.9 %convert_reduce_fusion = (f32[8,768]{1,0:T(8,128)S(1)}, bf16[128,768]{1,0:T(8,128)(2,1)}) fusion(bf16[128,768]{1,0:T(8,128)(2,1)} %reduce-scatter.2.cloned.1.call-done, f32[768]{0:T(1024)S(1)} %copy-done.4, f32[128,768]{1,0:T(8,128)S(1)} %get-tuple-element.7, f32[128]{0:T(128)S(1)} %rsqrt_bitcast_fusion), kind=kLoop, calls=%fused_computation.37 | loop fusion | flops 1665024 | bytes 814592 | tf_op jit(solution)/shard_map/reduce_sum | solution.py:150
  128.1 5.0 %psum.15 = bf16[8,256]{1,0:T(8,128)(2,1)S(1)} all-reduce(f32[8,256]{1,0:T(8,128)S(1)} %fusion.37), channel_id=1, replica_groups=mesh['grp'=2,'seq'=4,'tp'=2,'pr'=2] {'tp'}, use_global_device_ids=true, to_apply=%region_7.8 | all-reduce | flops 2048 | bytes 12288 | tf_op jit(solution)/shard_map/psum | solution.py:152
  133.1 14.1 %all_gather.35 = bf16[64,256]{1,0:T(8,128)(2,1)S(1)} all-gather(bf16[8,256]{1,0:T(8,128)(2,1)S(1)} %psum.15), channel_id=1, replica_groups=mesh['grp'=2,'seq'=4,'tp'=2,'pr'=2] {'seq','pr'}, dimensions={0}, use_global_device_ids=true | all-gather | bytes 36864 | tf_op jit(solution)/shard_map/all_gather | solution.py:153
  (64 shorter events, 6.3 us)
Async XLA Ops:
  7.2 120.7 %copy-start = (bf16[768,256]{1,0:T(8,128)(2,1)S(1)}, bf16[768,256]{1,0:T(8,128)(2,1)}, u32[]{:S(2)}) copy-start(bf16[768,256]{1,0:T(8,128)(2,1)} %param.21) | copy-start | bytes 1179652
  7.2 21.3 %all-gather.6.cloned.1.call-start = ((), (), s32[]{:S(2)}) async-start(), calls=%async_computation.5 | async-start | bytes 8847360 | tf_op jit(solution)/shard_map/all_gather | solution.py:96
  7.9 2.1 %copy-start.2 = (bf16[128,384]{1,0:T(8,128)(2,1)S(1)}, bf16[128,384]{1,0:T(8,128)(2,1)}, u32[]{:S(2)}) copy-start(bf16[128,384]{1,0:T(8,128)(2,1)} %param.13) | copy-start | bytes 294916
  7.9 40.7 %all-gather.12.cloned.1.call-start = ((), (), s32[]{:S(2)}) async-start(), calls=%async_computation.8 | async-start | bytes 2359296 | tf_op jit(solution)/shard_map/all_gather | solution.py:113
  8.7 47.7 %all-gather.8.cloned.1.call-start = ((), (), s32[]{:S(2)}) async-start(), calls=%async_computation.6 | async-start | bytes 3538944 | tf_op jit(solution)/shard_map/all_gather | solution.py:114
  9.4 57.8 %all-gather.10.cloned.1.call-start = ((), (), s32[]{:S(2)}) async-start(), calls=%async_computation.7 | async-start | bytes 2359296 | tf_op jit(solution)/shard_map/all_gather | solution.py:112
  10.0 100.9 %all-gather.14.cloned.1.call-start = ((), (), s32[]{:S(2)}) async-start(), calls=%async_computation.9 | async-start | bytes 3538944 | tf_op jit(solution)/shard_map/all_gather | solution.py:143
  10.1 3.8 %collective-permute-start = (bf16[2,384]{1,0:T(2,128)(2,1)S(1)}, bf16[2,384]{1,0:T(2,128)(2,1)S(1)}, u32[]{:S(2)}, u32[]{:S(2)}) collective-permute-start(bf16[2,384]{1,0:T(2,128)(2,1)S(1)} %get-tuple-element.4), channel_id=1, source_target_pairs={{0,1},{1,4},{4,5},{5,8},{8,9},{9,12},{12,13},{2,3},{3,6},{6,7},{7,... | collective-permute-start | bytes 4616 | tf_op jit(solution)/shard_map/ppermute | solution.py:30
  12.5 5.2 %collective-permute-start.1 = (bf16[2,384]{1,0:T(2,128)(2,1)S(1)}, bf16[2,384]{1,0:T(2,128)(2,1)S(1)}, u32[]{:S(2)}, u32[]{:S(2)}) collective-permute-start(bf16[2,384]{1,0:T(2,128)(2,1)S(1)} %get-tuple-element.5), channel_id=1, source_target_pairs={{1,0},{4,1},{5,4},{8,5},{9,8},{12,9},{13,12},{3,2},{6,3},{7,6},{10... | collective-permute-start | bytes 4616 | tf_op jit(solution)/shard_map/ppermute | solution.py:31
  33.3 8.3 %copy-start.4 = (f32[768]{0:T(1024)S(1)}, f32[768]{0:T(1024)}, u32[]{:S(2)}) copy-start(f32[768]{0:T(1024)} %param.15) | copy-start | bytes 9220
  34.9 13.7 %copy-start.3 = (f32[1536]{0:T(1024)S(1)}, f32[1536]{0:T(1024)}, u32[]{:S(2)}) copy-start(f32[1536]{0:T(1024)} %param.16) | copy-start | bytes 18436
  54.6 22.7 %collective-permute-start.2 = (bf16[256,2,128]{2,0,1:T(8,128)(2,1)S(1)}, bf16[256,2,128]{2,0,1:T(8,128)(2,1)S(1)}, u32[]{:S(2)}, u32[]{:S(2)}) collective-permute-start(bf16[256,2,128]{2,0,1:T(8,128)(2,1)S(1)} %bitcast.79), channel_id=1, source_target_pairs={{0,4},{4,8},{8,12},{12,0},{1,5},{5,9},{9,13},{13,1},{2,6},{6,10},{... | collective-permute-start | bytes 393224 | tf_op jit(solution)/shard_map/ppermute | solution.py:18
  73.8 23.9 %all-to-all-start.1 = ((bf16[128,4,128]{2,0,1:T(8,128)(2,1)}), bf16[128,4,128]{2,0,1:T(8,128)(2,1)S(1)}, u32[]{:S(2)}, u32[]{:S(2)}) async-start(bf16[128,4,128]{2,0,1:T(8,128)(2,1)} %bitcast.72), calls=%async_computation.1 | async-start | bytes 262144 | tf_op jit(solution)/shard_map/all_to_all | solution.py:125
  77.2 48.7 %reduce-scatter.2.cloned.1.call-start = ((), (), s32[]{:S(2)}) async-start(), calls=%async_computation.10 | async-start | bytes 589824 | tf_op jit(solution)/shard_map/reduce_scatter | solution.py:146
  77.3 20.5 %collective-permute-start.3 = (bf16[256,2,128]{2,0,1:T(8,128)(2,1)S(1)}, bf16[256,2,128]{2,0,1:T(8,128)(2,1)S(1)}, u32[]{:S(2)}, u32[]{:S(2)}) collective-permute-start(bf16[256,2,128]{2,0,1:T(8,128)(2,1)S(1)} %collective-permute-done.2), channel_id=1, source_target_pairs={{0,4},{4,8},{8,12},{12,0},{1,5},{5,9},{9,13},{13,1},{2,6},{6,10},{... | collective-permute-start | bytes 393224 | tf_op jit(solution)/shard_map/ppermute | solution.py:18
  97.8 7.0 %collective-permute-start.4 = (bf16[256,2,128]{2,0,1:T(8,128)(2,1)S(1)}, bf16[256,2,128]{2,0,1:T(8,128)(2,1)S(1)}, u32[]{:S(2)}, u32[]{:S(2)}) collective-permute-start(bf16[256,2,128]{2,0,1:T(8,128)(2,1)S(1)} %collective-permute-done.3), channel_id=1, source_target_pairs={{0,4},{4,8},{8,12},{12,0},{1,5},{5,9},{9,13},{13,1},{2,6},{6,10},{... | collective-permute-start | bytes 393224 | tf_op jit(solution)/shard_map/ppermute | solution.py:18
  110.9 36.3 %copy-start.1 = (bf16[8,32,128]{2,1,0:T(8,128)(2,1)S(1)}, bf16[8,32,128]{2,1,0:T(8,128)(2,1)}, u32[]{:S(2)}) copy-start(bf16[8,32,128]{2,1,0:T(8,128)(2,1)} %param.22) | copy-start | bytes 196612
  110.9 36.4 %copy-start.5 = (f32[128]{0:T(128)S(1)}, f32[128]{0:T(128)}, u32[]{:S(2)}) copy-start(f32[128]{0:T(128)} %param.23) | copy-start | bytes 1540
  111.0 36.5 %copy-start.6 = (bf16[256,128]{1,0:T(8,128)(2,1)S(1)}, bf16[256,128]{1,0:T(8,128)(2,1)}, u32[]{:S(2)}) copy-start(bf16[256,128]{1,0:T(8,128)(2,1)} %param.25) | copy-start | bytes 196612
  111.0 36.5 %copy-start.7 = (bf16[128,256]{1,0:T(8,128)(2,1)S(1)}, bf16[128,256]{1,0:T(8,128)(2,1)}, u32[]{:S(2)}) copy-start(bf16[128,256]{1,0:T(8,128)(2,1)} %param.24) | copy-start | bytes 196612
Sparse Core Ops, SparseCore 0:
  9.5 18.8 all-gather.5
  30.0 10.9 all-gather.11
  42.6 12.2 all-gather.7
  56.2 10.9 all-gather.9
  68.6 12.1 all-gather.13
  114.1 11.7 reduce-scatter.1
